TPU v7x, 256 devices: a whole 4x4x8 slice. The times are simulated.
256 devices in a mesh: wide: 16 (over z_lo, x, core), long: 16 (over y, z_hi).
Axes of the slice: x: 4, y: 4, z: 8 (z_hi: 4, z_lo: 2; z = z_hi * 2 + z_lo), core: 2. Of those that a mesh axis runs over, the one named last changes fastest.
Arguments:
- slab_vertices: float32 [3, 4096], P(None, 'wide'), may hold values from 0 to 1
- slab_elements: int32 [3, 8192], P(None, 'wide'), may hold values from 0 to 4095, as said below
- source_vertices: float32 [3, 16384], P(None, ('wide', 'long')), may hold values from 0 to 1
- source_elements: int32 [3, 32768], P(None, ('wide', 'long')), may hold values from 0 to 16383, as said below
- primal_basis: bfloat16 [32, 32768], P(None, ('wide', 'long')), may hold values from -12 to 12
- adjoint_basis: bfloat16 [32, 8192], P(None, 'wide'), may hold values from -24 to 24
Outputs:
- primal_image: float32 [32, 8192], P(None, ('wide', 'long'))
- adjoint_image: float32 [32, 32768], P(None, ('wide', 'long'))
Inputs may be any that keep to these rules, and one draw needn't show every extreme that they name: `slab_elements`: a slab triangle in columns b * 512 to (b + 1) * 512 - 1 names only vertices b * 256 to (b + 1) * 256 - 1; both ends of each such range are named. `source_elements`: a source triangle in columns b * 128 to (b + 1) * 128 - 1 names only vertices b * 64 to (b + 1) * 64 - 1; both ends of each such range are named.
All inputs are finite; a program needn't handle non-finite values.
Results may differ from a plain program's by a relative error of at most 0.0029.
Values may be sent and summed in bfloat16 or wider, within the bound.
A program may use at most 64 MiB of HBM per device.

v0:
```python
import math

import jax
import jax.numpy as jnp
from jax import lax
from jax.sharding import PartitionSpec as P

WAVENUMBER = 40.0
SOFTENING = 0.0004
AREA_WEIGHT = 0.05
FOUR_PI = 4.0 * math.pi


def geometry(vertices, elements, anchor):
    local_ids = elements - anchor
    corners = [jnp.take(vertices, local_ids[corner], axis=1) for corner in range(3)]
    centre = (corners[0] + corners[1] + corners[2]) / 3.0
    edge_one = corners[1] - corners[0]
    edge_two = corners[2] - corners[0]
    normal_x = edge_one[1] * edge_two[2] - edge_one[2] * edge_two[1]
    normal_y = edge_one[2] * edge_two[0] - edge_one[0] * edge_two[2]
    normal_z = edge_one[0] * edge_two[1] - edge_one[1] * edge_two[0]
    areas = 0.5 * jnp.sqrt(normal_x * normal_x + normal_y * normal_y + normal_z * normal_z)
    return jnp.concatenate([centre, areas[None, :]], axis=0)


def kernel_tile(targets, sources):
    spread = targets[0][:, None] - sources[0][None, :]
    square_sum = spread * spread
    for axis_id in range(1, 3):
        spread = targets[axis_id][:, None] - sources[axis_id][None, :]
        square_sum = square_sum + spread * spread
    radius = jnp.sqrt(
        square_sum + SOFTENING + AREA_WEIGHT * (targets[3][:, None] + sources[3][None, :])
    )
    weight = targets[3][:, None] * sources[3][None, :] / (FOUR_PI * radius)
    phases = WAVENUMBER * radius
    return (
        (weight * jnp.cos(phases)).astype(jnp.bfloat16),
        (weight * jnp.sin(phases)).astype(jnp.bfloat16),
    )


def pack_primal(columns):
    half_rows = columns.shape[0] // 2
    real_part = columns[:half_rows]
    imag_part = columns[half_rows:]
    return jnp.concatenate(
        [jnp.concatenate([real_part, -imag_part], 1), jnp.concatenate([imag_part, real_part], 1)], 0
    )


def pack_adjoint(row_block):
    half_rows = row_block.shape[0] // 2
    real_part = row_block[:half_rows]
    imag_part = row_block[half_rows:]
    return jnp.concatenate(
        [jnp.concatenate([real_part, imag_part], 1), jnp.concatenate([imag_part, -real_part], 1)], 0
    )


def primal_part(primal_pack, tile_real, tile_imag):
    stacked = jnp.concatenate([tile_real, tile_imag], 1)
    return lax.dot_general(
        primal_pack, stacked, (((1,), (1,)), ((), ())), preferred_element_type=jnp.float32
    )


def adjoint_part(adjoint_pack, tile_real, tile_imag):
    stacked = jnp.concatenate([tile_real, tile_imag], 0)
    return jnp.dot(adjoint_pack, stacked, preferred_element_type=jnp.float32)


def shards(
    slab_vertices, slab_elements, source_vertices, source_elements, primal_basis, adjoint_basis
):
    slab_width = slab_elements.shape[1]
    source_width = source_elements.shape[1]
    out_rows = primal_basis.shape[0]
    wide_at = lax.axis_index("wide")
    flat_at = wide_at * lax.axis_size("long") + lax.axis_index("long")
    slab_points = geometry(slab_vertices, slab_elements, wide_at * (slab_width // 2))
    source_points = geometry(source_vertices, source_elements, flat_at * (source_width // 2))
    all_slab = lax.all_gather(slab_points, "wide", axis=1, tiled=True)
    primal_pack = pack_primal(primal_basis)
    initial = (
        jnp.zeros((out_rows, source_width), jnp.float32),
        jnp.zeros((out_rows, all_slab.shape[1]), jnp.float32),
    )
    portion = lax.all_gather(adjoint_basis, "wide", axis=1, tiled=True)
    extent = portion.shape[1]
    stride = math.gcd(extent, 1024)

    def advance(block, state):
        adjoint_acc, primal_acc = state
        offset = block * stride
        points = lax.dynamic_slice_in_dim(all_slab, offset, stride, 1)
        row_block = lax.dynamic_slice_in_dim(portion, block * stride, stride, 1)
        tile_real, tile_imag = kernel_tile(points, source_points)
        primal_acc = lax.dynamic_update_slice_in_dim(
            primal_acc, primal_part(primal_pack, tile_real, tile_imag), offset, 1
        )
        adjoint_acc = adjoint_acc + adjoint_part(pack_adjoint(row_block), tile_real, tile_imag)
        return (adjoint_acc, primal_acc)

    adjoint_image, primal_acc = lax.fori_loop(0, extent // stride, advance, initial)
    primal_image = lax.psum_scatter(primal_acc, ("wide", "long"), scatter_dimension=1, tiled=True)
    return (primal_image, adjoint_image)


def solution(mesh):
    return jax.shard_map(
        shards,
        mesh=mesh,
        in_specs=(
            P(None, "wide"),
            P(None, "wide"),
            P(None, ("wide", "long")),
            P(None, ("wide", "long")),
            P(None, ("wide", "long")),
            P(None, "wide"),
        ),
        out_specs=(P(None, ("wide", "long")), P(None, ("wide", "long"))),
        check_vma=False,
    )
```

profile of v0, /device:TPU:32, one launch (start us, length us, event | category | flops | bytes accessed | tf_op | source)
XLA Modules:
  0.0 1602.4 jit_solution(10598250876209024342)
XLA Ops:
  7.2 0.7 broadcast_subtract_fusion
  8.0 0.7 broadcast_subtract_fusion.1
  8.8 0.7 slice_negate_fusion
  9.5 0.8 copy.36
  10.3 0.6 gather_fusion.5
  11.0 0.7 gather_fusion.4
  11.7 0.7 gather_fusion.3
  12.4 0.8 copy.30
  13.3 1.0 gather_fusion.2
  14.3 0.1 copy.35
  14.4 1.0 gather_fusion.1
  15.5 0.1 copy.33
  15.6 1.0 gather_fusion
  16.6 0.1 copy.31
  16.8 18.6 %all_gather.7 = f32[4,8192]{1,0:T(4,128)S(1)} all-gather(f32[4,512]{1,0:T(4,128)S(1)} %pad_maximum_fusion), channel_id=1, replica_groups=mesh['wide'=16,'long'=16] {'wide'}, dimensions={1}, use_global_device_ids=true | all-gather | bytes 139264 | tf_op jit(solution)/shard_map/all_gather | solution.py:84
  35.4 17.9 %all_gather.6 = bf16[32,8192]{1,0:T(8,128)(2,1)S(1)} all-gather(bf16[32,512]{1,0:T(8,128)(2,1)} %param.17), channel_id=1, replica_groups=mesh['wide'=16,'long'=16] {'wide'}, dimensions={1}, use_global_device_ids=true | all-gather | bytes 557056 | tf_op jit(solution)/shard_map/all_gather | solution.py:90
  53.4 29.8 %while.16 = (s32[]{:T(128)}, f32[32,128]{1,0:T(8,128)S(1)}, f32[32,8192]{1,0:T(8,128)S(1)}, bf16[32,8192]{1,0:T(8,128)(2,1)S(1)}, f32[4,8192]{1,0:T(4,128)S(1)},...) while((s32[]{:T(128)}, f32[32,128]{1,0:T(8,128)S(1)}, ...), condition=%wide.region_1.4_spmd.clone, body=%wide.region_0.3_spmd.clone.sunk | while | flops 38854664 | bytes 2069793 | solution.py:106
  53.4 0.1 fusion.33
  53.6 3.1 multiply_convert_fusion.3
  56.7 0.2 convolution_add_fusion.2
  56.9 0.2 fusion.35
  57.2 0.1 fusion.33
  57.3 3.1 multiply_convert_fusion.3
  60.4 0.2 convolution_add_fusion.2
  60.6 0.2 fusion.35
  60.9 0.1 fusion.33
  61.0 3.1 multiply_convert_fusion.3
  64.1 0.2 convolution_add_fusion.2
  64.3 0.2 fusion.35
  64.8 3.1 multiply_convert_fusion.3
  67.8 0.2 convolution_add_fusion.2
  68.1 0.2 fusion.35
  68.3 0.1 fusion.33
  68.5 3.1 multiply_convert_fusion.3
  71.6 0.2 convolution_add_fusion.2
  71.8 0.2 fusion.35
  72.2 3.1 multiply_convert_fusion.3
  75.3 0.2 convolution_add_fusion.2
  75.5 0.2 fusion.35
  75.9 3.1 multiply_convert_fusion.3
  79.0 0.2 convolution_add_fusion.2
  79.2 0.2 fusion.35
  79.6 3.1 multiply_convert_fusion.3
  82.7 0.2 convolution_add_fusion.2
  83.0 0.2 fusion.35
  83.2 2.7 copy.42
  85.9 1508.2 %reduce-scatter.4.cloned.1.call-done = f32[32,32]{1,0:T(8,128)} async-done(((f32[8192,32]{1,0:T(8,128)}), f32[32,32]{1,0:T(8,128)}) %reduce-scatter.4.cloned.1.call-update) | async-done | bytes 4112
  1594.1 1.4 copy.43
  (47 shorter events, 1.2 us)
Async XLA Ops:
  7.2 1587.0 %reduce-scatter.4.cloned.1.call-start = ((), (), s32[]{:S(2)}) async-start(), calls=%async_computation.1 | async-start | bytes 4210688
  83.2 2.7 copy-start
Sparse Core Ops, SparseCore 0:
  86.0 1508.0 reduce-scatter.3
where the time goes:
time: 1600 us
  waiting for transfers between devices  1510 us (94%)
  blocking collectives  36.5 us (2%)
  other arithmetic  27.1 us (2%)
    unnamed x2, waiting for transfers between devices  1510 us
  transfers between devices with their start and end apart: 1, of which 1 were waited for; matrix products, arithmetic and copies ran while one was open for 0% of the time, Pallas kernels for 0%

commit v1 on v0

v1 whole, which is shorter than its diff:
```python
import functools
import math

import jax
import jax.numpy as jnp
from jax import lax
from jax.experimental import pallas as pl
from jax.experimental.pallas import tpu as pltpu
from jax.sharding import PartitionSpec as P

WAVENUMBER = 40.0
SOFTENING = 0.0004
AREA_WEIGHT = 0.05
TURNS = WAVENUMBER / (2.0 * math.pi)
SCALE = TURNS * TURNS
WEIGHT = TURNS / (4.0 * math.pi)
ROUND = 12582912.0
ROOT2 = math.sqrt(2.0)
SIN = tuple(ROOT2 * c for c in (3.14158202, -5.16714279, 2.54189895, -0.55463599))
COS = tuple(ROOT2 * c for c in (0.99999995, -4.93479286, 4.05841191, -1.33188013, 0.21969673))
ROWS = 48
MESH = pl.DeviceIdType.MESH
F32 = jnp.float32
BF16 = jnp.bfloat16


def split3(x):
    one = x.astype(BF16).astype(F32)
    rest = x - one
    two = rest.astype(BF16).astype(F32)
    three = (rest - two).astype(BF16).astype(F32)
    return one, two, three


def points(padded, ids, anchor):
    count, width = padded.shape[1], ids.shape[1]
    parts = jnp.concatenate(split3(padded), axis=0).astype(BF16)
    rows = lax.broadcasted_iota(jnp.int32, (count, width), 0) + anchor
    corners = []
    for corner in range(3):
        chosen = jnp.where(rows == ids[corner : corner + 1, :], 1.0, 0.0).astype(BF16)
        found = jnp.dot(parts, chosen, preferred_element_type=F32)
        corners.append(found[0:8] + found[8:16] + found[16:24])
    centre = (corners[0] + corners[1] + corners[2]) * (1.0 / 3.0) - 0.5
    one = corners[1] - corners[0]
    two = corners[2] - corners[0]
    ox, oy, oz = one[0:1], one[1:2], one[2:3]
    tx, ty, tz = two[0:1], two[1:2], two[2:3]
    nx = oy * tz - oz * ty
    ny = oz * tx - ox * tz
    nz = ox * ty - oy * tx
    area = 0.5 * jnp.sqrt(nx * nx + ny * ny + nz * nz)
    square = centre * centre
    norm = square[0:1] + square[1:2] + square[2:3]
    return centre, area, norm


def tile_values(scaled, weight):
    inverse = lax.rsqrt(scaled)
    turns = scaled * inverse
    part = turns - ((turns + ROUND) - ROUND)
    square = part * part
    sine = SIN[3]
    for c in SIN[2::-1]:
        sine = sine * square + c
    sine = sine * part
    cosine = COS[4]
    for c in COS[3::-1]:
        cosine = cosine * square + c
    heavy = weight * inverse
    bent = heavy * sine
    return (heavy - bent * sine).astype(BF16), (bent * cosine).astype(BF16)


def kernel(
    nw, nl, sv, se, xv, xe, pb, ab, primal_out, adjoint_out,
    slab_pad, source_pad, source_rows, slab_rows, features, areas, adjoint_pack,
    gathered, primal_acc, adjoint_send, adjoint_recv, primal_send, primal_recv,
    gather_out, gather_in, adjoint_go, adjoint_in, primal_go, primal_in,
):
    wide_at = lax.axis_index("wide")
    long_at = lax.axis_index("long")
    slab_width = se.shape[1]
    source_width = xe.shape[1]
    blocks = slab_width // 128

    barrier = pltpu.get_barrier_semaphore()

    def greet_wide(k, carry):
        pl.semaphore_signal(
            barrier, inc=1, device_id=(lax.rem(wide_at + k, nw), long_at), device_id_type=MESH
        )
        return carry

    def greet_long(k, carry):
        pl.semaphore_signal(
            barrier, inc=1, device_id=(wide_at, lax.rem(long_at + k, nl)), device_id_type=MESH
        )
        return carry

    lax.fori_loop(1, nw, greet_wide, 0)
    lax.fori_loop(1, nl, greet_long, 0)

    source_pad[...] = jnp.zeros_like(source_pad)
    source_pad[0:3, :] = xv[...]
    anchor = (wide_at * nl + long_at) * (source_width // 2)
    centre, area, norm = points(source_pad[...], xe[...], anchor)
    for n, piece in enumerate(split3(centre * (-2.0 * SCALE))):
        source_rows[3 * n : 3 * n + 3, :] = piece[0:3]
    for n, piece in enumerate(split3(SCALE * (norm + AREA_WEIGHT * area))):
        source_rows[9 + n : 10 + n, :] = piece
    source_rows[12:13, :] = jnp.ones((1, source_width), F32)
    for n, piece in enumerate(split3(area)):
        source_rows[13 + n : 14 + n, :] = piece
    gathered[0, 0:32, :] = pb[...]
    gathered[0, 32:48, :] = source_rows[...].astype(BF16)

    pl.semaphore_wait(barrier, nw + nl - 2)

    def gather_copy(k):
        return pltpu.make_async_remote_copy(
            src_ref=gathered.at[0],
            dst_ref=gathered.at[k],
            send_sem=gather_out.at[k],
            recv_sem=gather_in.at[k],
            device_id=(lax.rem(wide_at + nw - k, nw), long_at),
            device_id_type=MESH,
        )

    def gather_start(k, carry):
        gather_copy(k).start()
        return carry

    lax.fori_loop(1, nw, gather_start, 0)

    slab_pad[...] = jnp.zeros_like(slab_pad)
    slab_pad[0:3, :] = sv[...]
    centre, area, norm = points(slab_pad[...], se[...], wide_at * (slab_width // 2))
    one, two, three = (piece[0:3] for piece in split3(centre))
    norms = split3(SCALE * (norm + SOFTENING + AREA_WEIGHT * area))
    slab_rows[...] = jnp.zeros_like(slab_rows)
    for n in range(3):
        slab_rows[3 * n : 3 * n + 3, :] = one
        slab_rows[9 + n : 10 + n, :] = jnp.ones((1, slab_width), F32)
        slab_rows[16 * n + 12 : 16 * n + 13, :] = norms[n]
    for n in range(2):
        slab_rows[16 + 3 * n : 19 + 3 * n, :] = two
    slab_rows[32:35, :] = three
    slab_rows[48:49, :] = WEIGHT * area
    turned = slab_rows[...].T
    features[...] = turned[:, 0:ROWS].astype(BF16)
    areas[...] = jnp.broadcast_to(turned[:, 48:49], areas.shape)

    rows = ab[...]
    crossed = jnp.concatenate([rows[16:32], -rows[0:16]], axis=0)
    for b in range(blocks):
        adjoint_pack[b, :, 0:128] = rows[:, 128 * b : 128 * b + 128]
        adjoint_pack[b, :, 128:256] = crossed[:, 128 * b : 128 * b + 128]
    primal_acc[...] = jnp.zeros_like(primal_acc)

    def adjoint_copy(k):
        return pltpu.make_async_remote_copy(
            src_ref=adjoint_send.at[k],
            dst_ref=adjoint_recv.at[k],
            send_sem=adjoint_go.at[k],
            recv_sem=adjoint_in.at[k],
            device_id=(lax.rem(wide_at + k, nw), long_at),
            device_id_type=MESH,
        )

    def step(k, carry):
        @pl.when(k > 0)
        def _():
            gather_copy(k).wait_recv()

        columns = gathered[k, 0:32, :]
        turned_columns = jnp.concatenate([-columns[16:32], columns[0:16]], axis=0)
        primal_pack = jnp.concatenate([columns, turned_columns], axis=1)
        source = gathered[k, 32:48, :]
        stacked = jnp.concatenate([source, source, source], axis=0)
        wide_source = source.astype(F32)
        source_area = wide_source[13:14] + wide_source[14:15] + wide_source[15:16]
        total = jnp.zeros((32, 128), F32)
        for b in range(blocks):
            distance = jnp.dot(
                features[128 * b : 128 * b + 128, :], stacked, preferred_element_type=F32
            )
            reals, imags = [], []
            for q in range(4):
                weight = areas[128 * b + 32 * q : 128 * b + 32 * q + 32, :] * source_area
                real, imag = tile_values(distance[32 * q : 32 * q + 32, :], weight)
                reals.append(real)
                imags.append(imag)
            real = jnp.concatenate(reals, axis=0)
            imag = jnp.concatenate(imags, axis=0)
            total = total + jnp.dot(
                adjoint_pack[b], jnp.concatenate([real, imag], axis=0), preferred_element_type=F32
            )
            primal_acc[:, 128 * b : 128 * b + 128] += lax.dot_general(
                primal_pack,
                jnp.concatenate([real, imag], axis=1),
                (((1,), (1,)), ((), ())),
                preferred_element_type=F32,
            )
        adjoint_send[k] = total

        @pl.when(k > 0)
        def _():
            adjoint_copy(k).start()

        return carry

    lax.fori_loop(0, nw, step, 0)

    lane = lax.broadcasted_iota(jnp.int32, (8, 128), 1) // 32
    for b in range(blocks):
        held = [primal_acc[8 * j : 8 * j + 8, 128 * b : 128 * b + 128] for j in range(4)]
        for q in range(4):
            piece = jnp.zeros((8, 128), F32)
            for j in range(4):
                shift = (32 * (j - q)) % 128
                moved = held[j] if shift == 0 else pltpu.roll(held[j], shift, 1)
                piece = jnp.where(lane == j, moved, piece)
            primal_send[4 * b + q] = piece

    def primal_copy(k):
        peer = lax.rem(long_at + k, nl)
        return pltpu.make_async_remote_copy(
            src_ref=primal_send.at[peer],
            dst_ref=primal_recv.at[k],
            send_sem=primal_go.at[k],
            recv_sem=primal_in.at[k],
            device_id=(wide_at, peer),
            device_id_type=MESH,
        )

    def primal_start(k, carry):
        primal_copy(k).start()
        return carry

    lax.fori_loop(1, nl, primal_start, 0)

    def adjoint_sum(k, total):
        adjoint_copy(k).wait_recv()
        return total + adjoint_recv[k]

    adjoint_out[...] = lax.fori_loop(1, nw, adjoint_sum, adjoint_send[0])

    def primal_sum(k, total):
        primal_copy(k).wait_recv()
        return total + primal_recv[k]

    total = lax.fori_loop(1, nl, primal_sum, primal_send[long_at])
    for j in range(4):
        primal_out[8 * j : 8 * j + 8, :] = total[:, 32 * j : 32 * j + 32]

    def finish_wide(k, carry):
        gather_copy(k).wait_send()
        adjoint_copy(k).wait_send()
        return carry

    def finish_long(k, carry):
        primal_copy(k).wait_send()
        return carry

    lax.fori_loop(1, nw, finish_wide, 0)
    lax.fori_loop(1, nl, finish_long, 0)


def solution(mesh):
    nw, nl = mesh.shape["wide"], mesh.shape["long"]

    def shards(sv, se, xv, xe, pb, ab):
        slab_width, source_width = se.shape[1], xe.shape[1]
        vmem = pl.BlockSpec(memory_space=pltpu.VMEM)
        return pl.pallas_call(
            functools.partial(kernel, nw, nl),
            out_shape=(
                jax.ShapeDtypeStruct((32, slab_width // nl), F32),
                jax.ShapeDtypeStruct((32, source_width), F32),
            ),
            in_specs=[vmem] * 6,
            out_specs=(vmem, vmem),
            scratch_shapes=[
                pltpu.VMEM((8, sv.shape[1]), F32),
                pltpu.VMEM((8, xv.shape[1]), F32),
                pltpu.VMEM((16, source_width), F32),
                pltpu.VMEM((64, slab_width), F32),
                pltpu.VMEM((slab_width, ROWS), BF16),
                pltpu.VMEM((slab_width, 128), F32),
                pltpu.VMEM((slab_width // 128, 32, 256), BF16),
                pltpu.VMEM((nw, ROWS, source_width), BF16),
                pltpu.VMEM((32, slab_width), F32),
                pltpu.VMEM((nw, 32, source_width), F32),
                pltpu.VMEM((nw, 32, source_width), F32),
                pltpu.VMEM((nl, 8, 128), F32),
                pltpu.VMEM((nl, 8, 128), F32),
                pltpu.SemaphoreType.DMA((nw,)),
                pltpu.SemaphoreType.DMA((nw,)),
                pltpu.SemaphoreType.DMA((nw,)),
                pltpu.SemaphoreType.DMA((nw,)),
                pltpu.SemaphoreType.DMA((nl,)),
                pltpu.SemaphoreType.DMA((nl,)),
            ],
            compiler_params=pltpu.CompilerParams(collective_id=0, has_side_effects=True),
        )(sv, se, xv, xe, pb, ab)

    return jax.shard_map(
        shards,
        mesh=mesh,
        in_specs=(
            P(None, "wide"),
            P(None, "wide"),
            P(None, ("wide", "long")),
            P(None, ("wide", "long")),
            P(None, ("wide", "long")),
            P(None, "wide"),
        ),
        out_specs=(P(None, ("wide", "long")), P(None, ("wide", "long"))),
        check_vma=False,
    )
```

time: 1600 us -> 35.7 us (0.02)
  the two profiles are of different devices: /device:TPU:32 before, /device:TPU:1 now
where the time goes in v1:
time: 35.7 us; the launch traced here: 35.5 us
  Pallas kernels  32.9 us (92%)
  local copies, waits for them, and re-layouts  1.94 us (5%)
  between operations  0.65 us (2%)
    pallas_call x1, Pallas kernels, shards(): pl.pallas_call(functools.partial(kernel, nw, nl), out_shape=(jax.ShapeDty...  32.9 us
    unnamed x4, local copies, waits for them, and re-layouts  1.94 us

profile of v1, /device:TPU:1, one launch (start us, length us, event | category | flops | bytes accessed | tf_op | source)
XLA Modules:
  0.0 35.5 jit_solution(9171451751600219958)
XLA Ops:
  0.6 32.9 %shard_map.77 = (f32[32,32]{1,0:T(8,128)}, f32[32,128]{1,0:T(8,128)}) custom-call(f32[3,256]{1,0:T(4,128)} %sv.1, s32[3,512]{1,0:T(4,128)} %se.1, f32[3,64]{1,0:T(4,128)} %xv.1, s32[3,128]{1,0:T(4,128)} %xe.1, bf16[32,128]{1,0:T(8,128)(2,1)} %pb.1, bf16[32,512]{1,0:T(8,128)(2,1)} %ab.1), custom_call_target="tpu_custom_call" | custom-call | tf_op jit(solution)/shard_map/pallas_call | solution.py:276
  33.5 0.0 copy-start
  33.5 1.3 %copy.10 = f32[32,32]{1,0:T(8,128)} copy(f32[32,32]{1,0:T(8,128)} %get-tuple-element.4) | data formatting | bytes 8192
  34.9 0.0 copy-done
  34.9 0.6 %copy.11 = f32[32,128]{1,0:T(8,128)} copy(f32[32,128]{1,0:T(8,128)S(1)} %copy-done) | data formatting | bytes 32768
Async XLA Ops:
  33.5 1.3 %copy-start = (f32[32,128]{1,0:T(8,128)S(1)}, f32[32,128]{1,0:T(8,128)}, u32[]{:S(2)}) copy-start(f32[32,128]{1,0:T(8,128)} %get-tuple-element.5) | copy-start | bytes 49156

commit v2 on v1

--- a/solution.py
+++ b/solution.py
@@ -19,6 +19,8 @@
 SIN = tuple(ROOT2 * c for c in (3.14158202, -5.16714279, 2.54189895, -0.55463599))
 COS = tuple(ROOT2 * c for c in (0.99999995, -4.93479286, 4.05841191, -1.33188013, 0.21969673))
 ROWS = 48
+GROUP = 3
+PIECE = 32
 MESH = pl.DeviceIdType.MESH
 F32 = jnp.float32
 BF16 = jnp.bfloat16
@@ -168,49 +170,69 @@
             device_id_type=MESH,
         )
 
-    def step(k, carry):
-        @pl.when(k > 0)
-        def _():
-            gather_copy(k).wait_recv()
-
+    def distances(k, b):
+        source = gathered[k, 32:48, :]
+        stacked = jnp.concatenate([source, source, source], axis=0)
+        return jnp.dot(
+            features[128 * b : 128 * b + 128, :], stacked, preferred_element_type=F32
+        )
+
+    def values(k, b, distance):
+        source = gathered[k, 32:48, :].astype(F32)
+        source_area = source[13:14] + source[14:15] + source[15:16]
+        reals, imags = [], []
+        for q in range(128 // PIECE):
+            at = 128 * b + PIECE * q
+            weight = areas[at : at + PIECE, :] * source_area
+            real, imag = tile_values(distance[PIECE * q : PIECE * q + PIECE, :], weight)
+            reals.append(real)
+            imags.append(imag)
+        return jnp.concatenate(reals, axis=0), jnp.concatenate(imags, axis=0)
+
+    def images(k, b, real, imag):
         columns = gathered[k, 0:32, :]
         turned_columns = jnp.concatenate([-columns[16:32], columns[0:16]], axis=0)
-        primal_pack = jnp.concatenate([columns, turned_columns], axis=1)
-        source = gathered[k, 32:48, :]
-        stacked = jnp.concatenate([source, source, source], axis=0)
-        wide_source = source.astype(F32)
-        source_area = wide_source[13:14] + wide_source[14:15] + wide_source[15:16]
-        total = jnp.zeros((32, 128), F32)
-        for b in range(blocks):
-            distance = jnp.dot(
-                features[128 * b : 128 * b + 128, :], stacked, preferred_element_type=F32
-            )
-            reals, imags = [], []
-            for q in range(4):
-                weight = areas[128 * b + 32 * q : 128 * b + 32 * q + 32, :] * source_area
-                real, imag = tile_values(distance[32 * q : 32 * q + 32, :], weight)
-                reals.append(real)
-                imags.append(imag)
-            real = jnp.concatenate(reals, axis=0)
-            imag = jnp.concatenate(imags, axis=0)
-            total = total + jnp.dot(
-                adjoint_pack[b], jnp.concatenate([real, imag], axis=0), preferred_element_type=F32
-            )
-            primal_acc[:, 128 * b : 128 * b + 128] += lax.dot_general(
-                primal_pack,
-                jnp.concatenate([real, imag], axis=1),
-                (((1,), (1,)), ((), ())),
-                preferred_element_type=F32,
-            )
-        adjoint_send[k] = total
-
-        @pl.when(k > 0)
-        def _():
-            adjoint_copy(k).start()
-
-        return carry
-
-    lax.fori_loop(0, nw, step, 0)
+        primal_acc[:, 128 * b : 128 * b + 128] += lax.dot_general(
+            jnp.concatenate([columns, turned_columns], axis=1),
+            jnp.concatenate([real, imag], axis=1),
+            (((1,), (1,)), ((), ())),
+            preferred_element_type=F32,
+        )
+        return jnp.dot(
+            adjoint_pack[b], jnp.concatenate([real, imag], axis=0), preferred_element_type=F32
+        )
+
+    def process(chunks):
+        todo = [(c, b) for c in range(len(chunks)) for b in range(blocks)]
+        totals = [jnp.zeros((32, 128), F32) for _ in chunks]
+        ahead = distances(chunks[0], 0)
+        behind = None
+        for n, (c, b) in enumerate(todo):
+            distance = ahead
+            if n + 1 < len(todo):
+                after, next_block = todo[n + 1]
+                ahead = distances(chunks[after], next_block)
+            if behind is not None:
+                old, old_block, pair = behind
+                totals[old] = totals[old] + images(chunks[old], old_block, *pair)
+            behind = (c, b, values(chunks[c], b, distance))
+        old, old_block, pair = behind
+        totals[old] = totals[old] + images(chunks[old], old_block, *pair)
+        for c, k in enumerate(chunks):
+            adjoint_send[k] = totals[c]
+
+    def step(g, carry):
+        first = 1 + g * GROUP
+
+        for c in range(GROUP):
+            gather_copy(first + c).wait_recv()
+        process([first + c for c in range(GROUP)])
+        for c in range(GROUP):
+            adjoint_copy(first + c).start()
+        return carry
+
+    process([0])
+    lax.fori_loop(0, (nw - 1) // GROUP, step, 0)
 
     lane = lax.broadcasted_iota(jnp.int32, (8, 128), 1) // 32
     for b in range(blocks):

time: 35.7 us -> 30.8 us (0.86)
  Pallas kernels: 32.9 us -> 28 us
    pallas_call x1, Pallas kernels: 32.9 us -> 28 us  [shards(): pl.pallas_call(functools.partial(kernel, nw, nl), out_shape=(jax.ShapeDty...]
where the time goes in v2:
time: 30.8 us; the launch traced here: 30.6 us
  Pallas kernels  28 us (91%)
  local copies, waits for them, and re-layouts  1.94 us (6%)
  between operations  0.65 us (2%)
    pallas_call x1, Pallas kernels, shards(): pl.pallas_call(functools.partial(kernel, nw, nl), out_shape=(jax.ShapeDty...  28 us
    unnamed x4, local copies, waits for them, and re-layouts  1.94 us

profile of v2, /device:TPU:1, one launch (start us, length us, event | category | flops | bytes accessed | tf_op | source)
XLA Modules:
  0.0 30.6 jit_solution(13918608790643840115)
XLA Ops:
  0.6 28.0 %shard_map.77 = (f32[32,32]{1,0:T(8,128)}, f32[32,128]{1,0:T(8,128)}) custom-call(f32[3,256]{1,0:T(4,128)} %sv.1, s32[3,512]{1,0:T(4,128)} %se.1, f32[3,64]{1,0:T(4,128)} %xv.1, s32[3,128]{1,0:T(4,128)} %xe.1, bf16[32,128]{1,0:T(8,128)(2,1)} %pb.1, bf16[32,512]{1,0:T(8,128)(2,1)} %ab.1), custom_call_target="tpu_custom_call" | custom-call | tf_op jit(solution)/shard_map/pallas_call | solution.py:298
  28.6 0.0 copy-start
  28.6 1.3 %copy.10 = f32[32,32]{1,0:T(8,128)} copy(f32[32,32]{1,0:T(8,128)} %get-tuple-element.4) | data formatting | bytes 8192
  29.9 0.0 copy-done
  30.0 0.6 %copy.11 = f32[32,128]{1,0:T(8,128)} copy(f32[32,128]{1,0:T(8,128)S(1)} %copy-done) | data formatting | bytes 32768
Async XLA Ops:
  28.6 1.3 %copy-start = (f32[32,128]{1,0:T(8,128)S(1)}, f32[32,128]{1,0:T(8,128)}, u32[]{:S(2)}) copy-start(f32[32,128]{1,0:T(8,128)} %get-tuple-element.5) | copy-start | bytes 49156

commit v3 on v2

--- a/solution.py
+++ b/solution.py
@@ -75,7 +75,8 @@
 
 
 def kernel(
-    nw, nl, sv, se, xv, xe, pb, ab, primal_out, adjoint_out,
+    nw, nl, sv_far, se_far, xv_far, xe_far, pb_far, ab_far, primal_out, adjoint_out,
+    sv, se, xv, xe, pb, ab, arrived,
     slab_pad, source_pad, source_rows, slab_rows, features, areas, adjoint_pack,
     gathered, primal_acc, adjoint_send, adjoint_recv, primal_send, primal_recv,
     gather_out, gather_in, adjoint_go, adjoint_in, primal_go, primal_in,
@@ -103,6 +104,17 @@
     lax.fori_loop(1, nw, greet_wide, 0)
     lax.fori_loop(1, nl, greet_long, 0)
 
+    fetches = [
+        pltpu.make_async_copy(far, near, arrived.at[n])
+        for n, (far, near) in enumerate(
+            ((xv_far, xv), (xe_far, xe), (pb_far, pb), (sv_far, sv), (se_far, se), (ab_far, ab))
+        )
+    ]
+    for fetch in fetches:
+        fetch.start()
+
+    for fetch in fetches[:3]:
+        fetch.wait()
     source_pad[...] = jnp.zeros_like(source_pad)
     source_pad[0:3, :] = xv[...]
     anchor = (wide_at * nl + long_at) * (source_width // 2)
@@ -135,6 +147,8 @@
 
     lax.fori_loop(1, nw, gather_start, 0)
 
+    for fetch in fetches[3:]:
+        fetch.wait()
     slab_pad[...] = jnp.zeros_like(slab_pad)
     slab_pad[0:3, :] = sv[...]
     centre, area, norm = points(slab_pad[...], se[...], wide_at * (slab_width // 2))
@@ -289,21 +303,33 @@
     lax.fori_loop(1, nl, finish_long, 0)
 
 
+def write_out(primal, adjoint, primal_out, adjoint_out, done):
+    one = pltpu.make_async_copy(primal, primal_out, done.at[0])
+    two = pltpu.make_async_copy(adjoint, adjoint_out, done.at[1])
+    one.start()
+    two.start()
+    one.wait()
+    two.wait()
+
+
 def solution(mesh):
     nw, nl = mesh.shape["wide"], mesh.shape["long"]
 
     def shards(sv, se, xv, xe, pb, ab):
         slab_width, source_width = se.shape[1], xe.shape[1]
+        far = pl.BlockSpec(memory_space=pl.ANY)
         vmem = pl.BlockSpec(memory_space=pltpu.VMEM)
-        return pl.pallas_call(
+        primal, adjoint = pl.pallas_call(
             functools.partial(kernel, nw, nl),
             out_shape=(
-                jax.ShapeDtypeStruct((32, slab_width // nl), F32),
-                jax.ShapeDtypeStruct((32, source_width), F32),
+                pltpu.VMEM((32, slab_width // nl), F32),
+                pltpu.VMEM((32, source_width), F32),
             ),
-            in_specs=[vmem] * 6,
+            in_specs=[far] * 6,
             out_specs=(vmem, vmem),
             scratch_shapes=[
+                *(pltpu.VMEM(x.shape, x.dtype) for x in (sv, se, xv, xe, pb, ab)),
+                pltpu.SemaphoreType.DMA((6,)),
                 pltpu.VMEM((8, sv.shape[1]), F32),
                 pltpu.VMEM((8, xv.shape[1]), F32),
                 pltpu.VMEM((16, source_width), F32),
@@ -326,6 +352,19 @@
             ],
             compiler_params=pltpu.CompilerParams(collective_id=0, has_side_effects=True),
         )(sv, se, xv, xe, pb, ab)
+        return pl.pallas_call(
+            write_out,
+            out_shape=(
+                jax.ShapeDtypeStruct(primal.shape, F32),
+                jax.ShapeDtypeStruct(adjoint.shape, F32),
+            ),
+            in_specs=[vmem, vmem],
+            out_specs=(far, far),
+            scratch_shapes=[pltpu.SemaphoreType.DMA((2,))],
+        )(
+            pltpu.with_memory_space_constraint(primal, pltpu.VMEM),
+            pltpu.with_memory_space_constraint(adjoint, pltpu.VMEM),
+        )
 
     return jax.shard_map(
         shards,

time: 30.8 us -> 28.3 us (0.919)
  local copies, waits for them, and re-layouts: 1.94 us -> 0 us
  Pallas kernels: 28 us -> 27.5 us
    unnamed x4 -> x0, local copies, waits for them, and re-layouts: 1.94 us -> none
    pallas_call x1 -> x2, Pallas kernels: 28 us -> 27.5 us  [the longest x1 26.8 us: shards(): pl.pallas_call(functools.partial(kernel, nw, nl), out_shape=(pltpu.VMEM((...]
where the time goes in v3:
time: 28.3 us; the launch traced here: 28.1 us
  Pallas kernels  27.5 us (97%)
  between operations  0.64 us (2%)
    pallas_call x1, Pallas kernels, shards(): pl.pallas_call(functools.partial(kernel, nw, nl), out_shape=(pltpu.VMEM((...  26.8 us
    pallas_call x1, Pallas kernels, shards(): pl.pallas_call(write_out, out_shape=(jax.ShapeDtypeStruct(primal.shape, F...  0.63 us

profile of v3, /device:TPU:1, one launch (start us, length us, event | category | flops | bytes accessed | tf_op | source)
XLA Modules:
  0.0 28.1 jit_solution(16875423358184140067)
XLA Ops:
  0.6 26.8 %shard_map.77 = (f32[32,32]{1,0:T(8,128)S(1)}, f32[32,128]{1,0:T(8,128)S(1)}) custom-call(f32[3,256]{1,0:T(4,128)} %sv_far.1, s32[3,512]{1,0:T(4,128)} %se_far.1, f32[3,64]{1,0:T(4,128)} %xv_far.1, s32[3,128]{1,0:T(4,128)} %xe_far.1, bf16[32,128]{1,0:T(8,128)(2,1)} %pb_far.1, bf16[32,512]{1,0:T(8,128)(2,1)} %ab_far.1), custom_call_target="tpu_custom_call" | custom-call | tf_op jit(solution)/shard_map/pallas_call | solution.py:322
  27.5 0.6 %shard_map.78 = (f32[32,32]{1,0:T(8,128)}, f32[32,128]{1,0:T(8,128)}) custom-call(f32[32,32]{1,0:T(8,128)S(1)} %get-tuple-element.4.primal, f32[32,128]{1,0:T(8,128)S(1)} %get-tuple-element.5.adjoint), custom_call_target="tpu_custom_call" | custom-call | tf_op jit(solution)/shard_map/pallas_call | solution.py:355

commit v4 on v3

--- a/solution.py
+++ b/solution.py
@@ -79,7 +79,7 @@
     sv, se, xv, xe, pb, ab, arrived,
     slab_pad, source_pad, source_rows, slab_rows, features, areas, adjoint_pack,
     gathered, primal_acc, adjoint_send, adjoint_recv, primal_send, primal_recv,
-    gather_out, gather_in, adjoint_go, adjoint_in, primal_go, primal_in,
+    gather_out, gather_in, adjoint_go, adjoint_in, primal_go, primal_in, known_y, known_z, known_all,
 ):
     wide_at = lax.axis_index("wide")
     long_at = lax.axis_index("long")
@@ -95,14 +95,19 @@
         )
         return carry
 
-    def greet_long(k, carry):
-        pl.semaphore_signal(
-            barrier, inc=1, device_id=(wide_at, lax.rem(long_at + k, nl)), device_id_type=MESH
-        )
-        return carry
+    def beside(step, size, by):
+        place = (long_at // step) % size
+        return long_at + ((place + by) % size - place) * step
+
+    def greet_ring(semaphore, step):
+        for by in (1, 3):
+            pl.semaphore_signal(
+                semaphore, inc=1, device_id=(wide_at, beside(step, 4, by)), device_id_type=MESH
+            )
 
     lax.fori_loop(1, nw, greet_wide, 0)
-    lax.fori_loop(1, nl, greet_long, 0)
+    greet_ring(barrier, 4)
+    greet_ring(barrier, 1)
 
     fetches = [
         pltpu.make_async_copy(far, near, arrived.at[n])
@@ -129,7 +134,7 @@
     gathered[0, 0:32, :] = pb[...]
     gathered[0, 32:48, :] = source_rows[...].astype(BF16)
 
-    pl.semaphore_wait(barrier, nw + nl - 2)
+    pl.semaphore_wait(barrier, nw - 1 + 4)
 
     def gather_copy(k):
         return pltpu.make_async_remote_copy(
@@ -146,6 +151,7 @@
         return carry
 
     lax.fori_loop(1, nw, gather_start, 0)
+    greet_ring(known_y, 4)
 
     for fetch in fetches[3:]:
         fetch.wait()
@@ -243,10 +249,23 @@
         process([first + c for c in range(GROUP)])
         for c in range(GROUP):
             adjoint_copy(first + c).start()
+
+        @pl.when(g == 0)
+        def _():
+            pl.semaphore_wait(known_y, 2)
+            greet_ring(known_z, 1)
+
+        @pl.when(g == 2)
+        def _():
+            pl.semaphore_wait(known_z, 2)
+            greet_ring(known_all, 1)
+
         return carry
 
     process([0])
     lax.fori_loop(0, (nw - 1) // GROUP, step, 0)
+
+    pl.semaphore_wait(known_all, 2)
 
     lane = lax.broadcasted_iota(jnp.int32, (8, 128), 1) // 32
     for b in range(blocks):
@@ -349,6 +368,9 @@
                 pltpu.SemaphoreType.DMA((nw,)),
                 pltpu.SemaphoreType.DMA((nl,)),
                 pltpu.SemaphoreType.DMA((nl,)),
+                pltpu.SemaphoreType.REGULAR,
+                pltpu.SemaphoreType.REGULAR,
+                pltpu.SemaphoreType.REGULAR,
             ],
             compiler_params=pltpu.CompilerParams(collective_id=0, has_side_effects=True),
         )(sv, se, xv, xe, pb, ab)

time: 28.3 us -> 27.4 us (0.968)
  Pallas kernels: 27.5 us -> 26.6 us
    pallas_call x1, Pallas kernels: 26.8 us -> 26 us  [shards(): pl.pallas_call(functools.partial(kernel, nw, nl), out_shape=(pltpu.VMEM((...]
where the time goes in v4:
time: 27.4 us; the launch traced here: 27.3 us
  Pallas kernels  26.6 us (97%)
  between operations  0.64 us (2%)
    pallas_call x1, Pallas kernels, shards(): pl.pallas_call(functools.partial(kernel, nw, nl), out_shape=(pltpu.VMEM((...  26 us
    pallas_call x1, Pallas kernels, shards(): pl.pallas_call(write_out, out_shape=(jax.ShapeDtypeStruct(primal.shape, F...  0.63 us

profile of v4, /device:TPU:1, one launch (start us, length us, event | category | flops | bytes accessed | tf_op | source)
XLA Modules:
  0.0 27.3 jit_solution(13350521039575124872)
XLA Ops:
  0.6 26.0 %shard_map.77 = (f32[32,32]{1,0:T(8,128)S(1)}, f32[32,128]{1,0:T(8,128)S(1)}) custom-call(f32[3,256]{1,0:T(4,128)} %sv_far.1, s32[3,512]{1,0:T(4,128)} %se_far.1, f32[3,64]{1,0:T(4,128)} %xv_far.1, s32[3,128]{1,0:T(4,128)} %xe_far.1, bf16[32,128]{1,0:T(8,128)(2,1)} %pb_far.1, bf16[32,512]{1,0:T(8,128)(2,1)} %ab_far.1), custom_call_target="tpu_custom_call" | custom-call | tf_op jit(solution)/shard_map/pallas_call | solution.py:341
  26.6 0.6 %shard_map.78 = (f32[32,32]{1,0:T(8,128)}, f32[32,128]{1,0:T(8,128)}) custom-call(f32[32,32]{1,0:T(8,128)S(1)} %get-tuple-element.4.primal, f32[32,128]{1,0:T(8,128)S(1)} %get-tuple-element.5.adjoint), custom_call_target="tpu_custom_call" | custom-call | tf_op jit(solution)/shard_map/pallas_call | solution.py:377

commit v5 on v4

--- a/solution.py
+++ b/solution.py
@@ -20,6 +20,7 @@
 COS = tuple(ROOT2 * c for c in (0.99999995, -4.93479286, 4.05841191, -1.33188013, 0.21969673))
 ROWS = 48
 GROUP = 3
+EARLY = 3
 PIECE = 32
 MESH = pl.DeviceIdType.MESH
 F32 = jnp.float32
@@ -190,20 +191,22 @@
             device_id_type=MESH,
         )
 
+    def at_block(b, start=0, size=128):
+        if isinstance(b, int):
+            return pl.ds(128 * b + start, size)
+        return pl.ds(pl.multiple_of(128 * b + start, size), size)
+
     def distances(k, b):
         source = gathered[k, 32:48, :]
         stacked = jnp.concatenate([source, source, source], axis=0)
-        return jnp.dot(
-            features[128 * b : 128 * b + 128, :], stacked, preferred_element_type=F32
-        )
+        return jnp.dot(features[at_block(b), :], stacked, preferred_element_type=F32)
 
     def values(k, b, distance):
         source = gathered[k, 32:48, :].astype(F32)
         source_area = source[13:14] + source[14:15] + source[15:16]
         reals, imags = [], []
         for q in range(128 // PIECE):
-            at = 128 * b + PIECE * q
-            weight = areas[at : at + PIECE, :] * source_area
+            weight = areas[at_block(b, PIECE * q, PIECE), :] * source_area
             real, imag = tile_values(distance[PIECE * q : PIECE * q + PIECE, :], weight)
             reals.append(real)
             imags.append(imag)
@@ -212,7 +215,7 @@
     def images(k, b, real, imag):
         columns = gathered[k, 0:32, :]
         turned_columns = jnp.concatenate([-columns[16:32], columns[0:16]], axis=0)
-        primal_acc[:, 128 * b : 128 * b + 128] += lax.dot_general(
+        primal_acc[:, at_block(b)] += lax.dot_general(
             jnp.concatenate([columns, turned_columns], axis=1),
             jnp.concatenate([real, imag], axis=1),
             (((1,), (1,)), ((), ())),
@@ -222,61 +225,57 @@
             adjoint_pack[b], jnp.concatenate([real, imag], axis=0), preferred_element_type=F32
         )
 
-    def process(chunks):
-        todo = [(c, b) for c in range(len(chunks)) for b in range(blocks)]
-        totals = [jnp.zeros((32, 128), F32) for _ in chunks]
-        ahead = distances(chunks[0], 0)
+    def process(todo, chunks):
+        totals = {}
+        ahead = distances(*todo[0])
         behind = None
-        for n, (c, b) in enumerate(todo):
+
+        def finish(k, b, pair):
+            term = images(k, b, *pair)
+            name = chunks[id(k)]
+            totals[name] = term if name not in totals else totals[name] + term
+
+        for n, (k, b) in enumerate(todo):
             distance = ahead
             if n + 1 < len(todo):
-                after, next_block = todo[n + 1]
-                ahead = distances(chunks[after], next_block)
+                ahead = distances(*todo[n + 1])
             if behind is not None:
-                old, old_block, pair = behind
-                totals[old] = totals[old] + images(chunks[old], old_block, *pair)
-            behind = (c, b, values(chunks[c], b, distance))
-        old, old_block, pair = behind
-        totals[old] = totals[old] + images(chunks[old], old_block, *pair)
-        for c, k in enumerate(chunks):
-            adjoint_send[k] = totals[c]
+                finish(*behind)
+            behind = (k, b, values(k, b, distance))
+        finish(*behind)
+        return totals
+
+    def by_chunk(slots):
+        chunks = {id(k): n for n, k in enumerate(slots)}
+        totals = process([(k, b) for k in slots for b in range(blocks)], chunks)
+        for n, k in enumerate(slots):
+            adjoint_send[k] = totals[n]
 
     def step(g, carry):
         first = 1 + g * GROUP
-
         for c in range(GROUP):
             gather_copy(first + c).wait_recv()
-        process([first + c for c in range(GROUP)])
+        by_chunk([first + c for c in range(GROUP)])
         for c in range(GROUP):
             adjoint_copy(first + c).start()
 
         @pl.when(g == 0)
-        def _():
-            pl.semaphore_wait(known_y, 2)
-            greet_ring(known_z, 1)
-
-        @pl.when(g == 2)
         def _():
             pl.semaphore_wait(known_z, 2)
             greet_ring(known_all, 1)
 
         return carry
 
-    process([0])
-    lax.fori_loop(0, (nw - 1) // GROUP, step, 0)
-
-    pl.semaphore_wait(known_all, 2)
-
+    by_chunk([0])
+    pl.semaphore_wait(known_y, 2)
+    greet_ring(known_z, 1)
+    lax.fori_loop(0, EARLY, step, 0)
+
+    rest = list(range(1 + EARLY * GROUP, nw))
+    for k in rest:
+        gather_copy(k).wait_recv()
+        adjoint_send[k] = jnp.zeros((32, 128), F32)
     lane = lax.broadcasted_iota(jnp.int32, (8, 128), 1) // 32
-    for b in range(blocks):
-        held = [primal_acc[8 * j : 8 * j + 8, 128 * b : 128 * b + 128] for j in range(4)]
-        for q in range(4):
-            piece = jnp.zeros((8, 128), F32)
-            for j in range(4):
-                shift = (32 * (j - q)) % 128
-                moved = held[j] if shift == 0 else pltpu.roll(held[j], shift, 1)
-                piece = jnp.where(lane == j, moved, piece)
-            primal_send[4 * b + q] = piece
 
     def primal_copy(k):
         peer = lax.rem(long_at + k, nl)
@@ -289,11 +288,36 @@
             device_id_type=MESH,
         )
 
-    def primal_start(k, carry):
-        primal_copy(k).start()
-        return carry
-
-    lax.fori_loop(1, nl, primal_start, 0)
+    def block_step(b, carry):
+        totals = process([(k, b) for k in rest], {id(k): k for k in rest})
+        for k in rest:
+            adjoint_send[k] += totals[k]
+
+        held = [primal_acc[8 * j : 8 * j + 8, at_block(b)] for j in range(4)]
+        for q in range(4):
+            piece = jnp.zeros((8, 128), F32)
+            for j in range(4):
+                shift = (32 * (j - q)) % 128
+                moved = held[j] if shift == 0 else pltpu.roll(held[j], shift, 1)
+                piece = jnp.where(lane == j, moved, piece)
+            primal_send[4 * b + q] = piece
+
+        @pl.when(b == 0)
+        def _():
+            pl.semaphore_wait(known_all, 2)
+
+        for q in range(4):
+            ahead = lax.rem(4 * b + q + nl - long_at, nl)
+
+            @pl.when(ahead > 0)
+            def _():
+                primal_copy(ahead).start()
+
+        return carry
+
+    lax.fori_loop(0, blocks, block_step, 0)
+    for k in rest:
+        adjoint_copy(k).start()
 
     def adjoint_sum(k, total):
         adjoint_copy(k).wait_recv()

time: 27.4 us -> 25.8 us (0.942)
  Pallas kernels: 26.6 us -> 25 us
    pallas_call x1, Pallas kernels: 26 us -> 24.4 us  [shards(): pl.pallas_call(functools.partial(kernel, nw, nl), out_shape=(pltpu.VMEM((...]
where the time goes in v5:
time: 25.8 us; the launch traced here: 25.6 us
  Pallas kernels  25 us (97%)
  between operations  0.64 us (2%)
    pallas_call x1, Pallas kernels, shards(): pl.pallas_call(functools.partial(kernel, nw, nl), out_shape=(pltpu.VMEM((...  24.4 us
    pallas_call x1, Pallas kernels, shards(): pl.pallas_call(write_out, out_shape=(jax.ShapeDtypeStruct(primal.shape, F...  0.63 us

profile of v5, /device:TPU:1, one launch (start us, length us, event | category | flops | bytes accessed | tf_op | source)
XLA Modules:
  0.0 25.6 jit_solution(15152968305166956160)
XLA Ops:
  0.6 24.4 %shard_map.77 = (f32[32,32]{1,0:T(8,128)S(1)}, f32[32,128]{1,0:T(8,128)S(1)}) custom-call(f32[3,256]{1,0:T(4,128)} %sv_far.1, s32[3,512]{1,0:T(4,128)} %se_far.1, f32[3,64]{1,0:T(4,128)} %xv_far.1, s32[3,128]{1,0:T(4,128)} %xe_far.1, bf16[32,128]{1,0:T(8,128)(2,1)} %pb_far.1, bf16[32,512]{1,0:T(8,128)(2,1)} %ab_far.1), custom_call_target="tpu_custom_call" | custom-call | tf_op jit(solution)/shard_map/pallas_call | solution.py:365
  25.0 0.6 %shard_map.78 = (f32[32,32]{1,0:T(8,128)}, f32[32,128]{1,0:T(8,128)}) custom-call(f32[32,32]{1,0:T(8,128)S(1)} %get-tuple-element.4.primal, f32[32,128]{1,0:T(8,128)S(1)} %get-tuple-element.5.adjoint), custom_call_target="tpu_custom_call" | custom-call | tf_op jit(solution)/shard_map/pallas_call | solution.py:401

commit v6 on v5

--- a/solution.py
+++ b/solution.py
@@ -19,8 +19,8 @@
 SIN = tuple(ROOT2 * c for c in (3.14158202, -5.16714279, 2.54189895, -0.55463599))
 COS = tuple(ROOT2 * c for c in (0.99999995, -4.93479286, 4.05841191, -1.33188013, 0.21969673))
 ROWS = 48
-GROUP = 3
-EARLY = 3
+
+
 PIECE = 32
 MESH = pl.DeviceIdType.MESH
 F32 = jnp.float32
@@ -251,27 +251,22 @@
         for n, k in enumerate(slots):
             adjoint_send[k] = totals[n]
 
-    def step(g, carry):
-        first = 1 + g * GROUP
-        for c in range(GROUP):
-            gather_copy(first + c).wait_recv()
-        by_chunk([first + c for c in range(GROUP)])
-        for c in range(GROUP):
-            adjoint_copy(first + c).start()
-
-        @pl.when(g == 0)
-        def _():
-            pl.semaphore_wait(known_z, 2)
-            greet_ring(known_all, 1)
-
-        return carry
+    def early(slots):
+        for k in slots:
+            gather_copy(k).wait_recv()
+        by_chunk(slots)
+        for k in slots:
+            adjoint_copy(k).start()
 
     by_chunk([0])
     pl.semaphore_wait(known_y, 2)
     greet_ring(known_z, 1)
-    lax.fori_loop(0, EARLY, step, 0)
-
-    rest = list(range(1 + EARLY * GROUP, nw))
+    early([1, 2, 3])
+    pl.semaphore_wait(known_z, 2)
+    greet_ring(known_all, 1)
+    early([4, 5, 6, 7, 8])
+
+    rest = list(range(9, nw))
     for k in rest:
         gather_copy(k).wait_recv()
         adjoint_send[k] = jnp.zeros((32, 128), F32)
@@ -319,19 +314,11 @@
     for k in rest:
         adjoint_copy(k).start()
 
-    def adjoint_sum(k, total):
+    total = adjoint_send[0]
+    for k in range(1, nw):
         adjoint_copy(k).wait_recv()
-        return total + adjoint_recv[k]
-
-    adjoint_out[...] = lax.fori_loop(1, nw, adjoint_sum, adjoint_send[0])
-
-    def primal_sum(k, total):
-        primal_copy(k).wait_recv()
-        return total + primal_recv[k]
-
-    total = lax.fori_loop(1, nl, primal_sum, primal_send[long_at])
-    for j in range(4):
-        primal_out[8 * j : 8 * j + 8, :] = total[:, 32 * j : 32 * j + 32]
+        total = total + adjoint_recv[k]
+    adjoint_out[...] = total
 
     def finish_wide(k, carry):
         gather_copy(k).wait_send()
@@ -344,6 +331,13 @@
 
     lax.fori_loop(1, nw, finish_wide, 0)
     lax.fori_loop(1, nl, finish_long, 0)
+
+    total = primal_send[long_at]
+    for k in range(1, nl):
+        primal_copy(k).wait_recv()
+        total = total + primal_recv[k]
+    for j in range(4):
+        primal_out[8 * j : 8 * j + 8, :] = total[:, 32 * j : 32 * j + 32]
 
 
 def write_out(primal, adjoint, primal_out, adjoint_out, done):

time: 25.8 us -> 25.4 us (0.984)
  Pallas kernels: 25 us -> 24.6 us
    pallas_call x1, Pallas kernels: 24.4 us -> 24 us  [shards(): pl.pallas_call(functools.partial(kernel, nw, nl), out_shape=(pltpu.VMEM((...]
where the time goes in v6:
time: 25.4 us; the launch traced here: 25.3 us
  Pallas kernels  24.6 us (97%)
  between operations  0.64 us (3%)
    pallas_call x1, Pallas kernels, shards(): pl.pallas_call(functools.partial(kernel, nw, nl), out_shape=(pltpu.VMEM((...  24 us
    pallas_call x1, Pallas kernels, shards(): pl.pallas_call(write_out, out_shape=(jax.ShapeDtypeStruct(primal.shape, F...  0.63 us

profile of v6, /device:TPU:1, one launch (start us, length us, event | category | flops | bytes accessed | tf_op | source)
XLA Modules:
  0.0 25.3 jit_solution(9293856849215307366)
XLA Ops:
  0.6 24.0 %shard_map.77 = (f32[32,32]{1,0:T(8,128)S(1)}, f32[32,128]{1,0:T(8,128)S(1)}) custom-call(f32[3,256]{1,0:T(4,128)} %sv_far.1, s32[3,512]{1,0:T(4,128)} %se_far.1, f32[3,64]{1,0:T(4,128)} %xv_far.1, s32[3,128]{1,0:T(4,128)} %xe_far.1, bf16[32,128]{1,0:T(8,128)(2,1)} %pb_far.1, bf16[32,512]{1,0:T(8,128)(2,1)} %ab_far.1), custom_call_target="tpu_custom_call" | custom-call | tf_op jit(solution)/shard_map/pallas_call | solution.py:359
  24.6 0.6 %shard_map.78 = (f32[32,32]{1,0:T(8,128)}, f32[32,128]{1,0:T(8,128)}) custom-call(f32[32,32]{1,0:T(8,128)S(1)} %get-tuple-element.4.primal, f32[32,128]{1,0:T(8,128)S(1)} %get-tuple-element.5.adjoint), custom_call_target="tpu_custom_call" | custom-call | tf_op jit(solution)/shard_map/pallas_call | solution.py:395

commit v7 on v6

--- a/solution.py
+++ b/solution.py
@@ -283,7 +283,8 @@
             device_id_type=MESH,
         )
 
-    def block_step(b, carry):
+    def block_step(n, carry):
+        b = n + (n // 2) * (1 - 2 * (n % 2))
         totals = process([(k, b) for k in rest], {id(k): k for k in rest})
         for k in rest:
             adjoint_send[k] += totals[k]

time: 25.4 us -> 25.5 us (level)
  no operation moved by 1% of the time
where the time goes in v7:
time: 25.5 us; the launch traced here: 25.3 us
  Pallas kernels  24.7 us (97%)
  between operations  0.64 us (3%)
    pallas_call x1, Pallas kernels, shards(): pl.pallas_call(functools.partial(kernel, nw, nl), out_shape=(pltpu.VMEM((...  24 us
    pallas_call x1, Pallas kernels, shards(): pl.pallas_call(write_out, out_shape=(jax.ShapeDtypeStruct(primal.shape, F...  0.63 us

profile of v7, /device:TPU:1, one launch (start us, length us, event | category | flops | bytes accessed | tf_op | source)
XLA Modules:
  0.0 25.3 jit_solution(14415074697627236636)
XLA Ops:
  0.6 24.0 %shard_map.77 = (f32[32,32]{1,0:T(8,128)S(1)}, f32[32,128]{1,0:T(8,128)S(1)}) custom-call(f32[3,256]{1,0:T(4,128)} %sv_far.1, s32[3,512]{1,0:T(4,128)} %se_far.1, f32[3,64]{1,0:T(4,128)} %xv_far.1, s32[3,128]{1,0:T(4,128)} %xe_far.1, bf16[32,128]{1,0:T(8,128)(2,1)} %pb_far.1, bf16[32,512]{1,0:T(8,128)(2,1)} %ab_far.1), custom_call_target="tpu_custom_call" | custom-call | tf_op jit(solution)/shard_map/pallas_call | solution.py:360
  24.7 0.6 %shard_map.78 = (f32[32,32]{1,0:T(8,128)}, f32[32,128]{1,0:T(8,128)}) custom-call(f32[32,32]{1,0:T(8,128)S(1)} %get-tuple-element.4.primal, f32[32,128]{1,0:T(8,128)S(1)} %get-tuple-element.5.adjoint), custom_call_target="tpu_custom_call" | custom-call | tf_op jit(solution)/shard_map/pallas_call | solution.py:396
